TPU v7x, 32 devices: a whole 2x2x4 slice. The times are simulated.
32 devices in a mesh: vp: 4 (over y, x), cp: 2 (over core), ga: 4 (over z).
Axes of the slice: x: 2, y: 2, z: 4, core: 2. Of those that a mesh axis runs over, the one named last changes fastest.
Arguments:
- valence_wavefunction: bfloat16 [512, 24576], P(('vp', 'cp'), 'ga'), may hold values from -6 to 6
- cond_wave: bfloat16 [512, 24576], P(('vp', 'cp'), 'ga'), may hold values from -6 to 6
- screen_basis: bfloat16 [24576, 1024], P('ga'), may hold values from -0.0390625 to 0.0390625
- screen: float32 [1024], replicated, may hold values from 0.01 to 0.1
- coulomb: float32 [1024], replicated, may hold values from 0.02 to 0.2
- window_rows: int32 [2], replicated, may hold values from 0 to 1023
- tile_owner: int32 [48], P(('vp', 'cp')), may hold values from 0 to 4095, as said below
Outputs:
- kernel: float32 [2, 48, 4096], P(None, ('vp', 'cp'), 'ga')
Inputs may be any that keep to these rules, and one draw needn't show every extreme that they name: `tile_owner`: distinct pair-block indices; 0 and 4095 both occur.
All inputs are finite; a program needn't handle non-finite values.
Results may differ from a plain program's by a relative error of at most 0.02.
Values may be sent and summed in bfloat16 or wider, within the bound.
A program may use at most 64 MiB of HBM per device.

v0:
```python
import jax
import jax.numpy as jnp
from jax import lax
from jax.sharding import PartitionSpec as P

R = 1024
TV = 8
TC = 8
NCT = 64


def select_bands(wanted, shard_part):
    row_ids = jnp.arange(shard_part.shape[0], dtype=jnp.int32)
    chooser = (wanted[:, None] == row_ids[None, :]).astype(jnp.bfloat16)
    return jnp.dot(chooser, shard_part, preferred_element_type=jnp.float32)


def outer_rows(left_wavefunction, right_wave):
    product = (
        left_wavefunction.astype(jnp.float32)[..., :, None, :]
        * right_wave.astype(jnp.float32)[..., None, :, :]
    )
    return product.astype(jnp.bfloat16)


def contract(row_proj, col_proj, val_proj, cond_proj, screen_part, coulomb_part):
    exchange_term = jnp.einsum(
        "qacr,svdr->qsacvd", row_proj * coulomb_part, col_proj, precision=lax.Precision.HIGHEST
    )
    direct_term = jnp.einsum(
        "qsavr,qscdr->qsacvd", val_proj * screen_part, cond_proj, precision=lax.Precision.HIGHEST
    )
    total = 2.0 * exchange_term - direct_term
    return total.reshape(total.shape[0], total.shape[1], -1)


def shards(valence_wavefunction, cond_wave, screen_basis, screen, coulomb, window_rows, tile_owner):
    slot_count = tile_owner.shape[0]
    grid_count = valence_wavefunction.shape[1]
    pair_tiles = jnp.concatenate([window_rows, tile_owner])
    val_wanted = (
        (pair_tiles // NCT)[:, None] * TV + jnp.arange(TV, dtype=jnp.int32)[None, :]
    ).reshape(-1)
    conduction_wanted = (
        (pair_tiles % NCT)[:, None] * TC + jnp.arange(TC, dtype=jnp.int32)[None, :]
    ).reshape(-1)
    picked_val = select_bands(
        val_wanted, lax.all_gather(valence_wavefunction, ("vp", "cp"), axis=0, tiled=True)
    )
    picked_cond = select_bands(
        conduction_wanted, lax.all_gather(cond_wave, ("vp", "cp"), axis=0, tiled=True)
    )
    picked_val = picked_val.astype(jnp.bfloat16).reshape(2 + slot_count, TV, grid_count)
    picked_cond = picked_cond.astype(jnp.bfloat16).reshape(2 + slot_count, TC, grid_count)
    row_val = picked_val[:2]
    slot_valence = picked_val[2:]
    row_cond = picked_cond[:2]
    slot_cond = picked_cond[2:]
    row_rho = outer_rows(row_val, row_cond).reshape(2 * TV * TC, grid_count)
    col_rho = outer_rows(slot_valence, slot_cond).reshape(slot_count * TV * TC, grid_count)
    val_rho = outer_rows(row_val[:, None], slot_valence[None]).reshape(
        2 * slot_count * TV * TV, grid_count
    )
    cond_rho = outer_rows(row_cond[:, None], slot_cond[None]).reshape(
        2 * slot_count * TC * TC, grid_count
    )
    row_part = jnp.dot(row_rho, screen_basis, preferred_element_type=jnp.float32)
    col_part = jnp.dot(col_rho, screen_basis, preferred_element_type=jnp.float32)
    val_part = jnp.dot(val_rho, screen_basis, preferred_element_type=jnp.float32)
    cond_part = jnp.dot(cond_rho, screen_basis, preferred_element_type=jnp.float32)
    live_tile = (tile_owner[None, :] >= window_rows[:, None])[:, :, None]
    grid_groups = lax.axis_size("ga")
    rank_span = R // grid_groups
    rank_first = lax.axis_index("ga") * rank_span
    row_sum, col_sum, val_sum, cond_sum = (
        lax.psum_scatter(
            row_part.astype(jnp.bfloat16), "ga", scatter_dimension=1, tiled=True
        ).astype(jnp.float32),
        lax.psum_scatter(
            col_part.astype(jnp.bfloat16), "ga", scatter_dimension=1, tiled=True
        ).astype(jnp.float32),
        lax.psum_scatter(
            val_part.astype(jnp.bfloat16), "ga", scatter_dimension=1, tiled=True
        ).astype(jnp.float32),
        lax.psum_scatter(
            cond_part.astype(jnp.bfloat16), "ga", scatter_dimension=1, tiled=True
        ).astype(jnp.float32),
    )
    screen_part = lax.dynamic_slice_in_dim(screen, rank_first, rank_span, 0)
    coulomb_part = lax.dynamic_slice_in_dim(coulomb, rank_first, rank_span, 0)
    kernel = contract(
        row_sum.reshape(2, TV, TC, rank_span),
        col_sum.reshape(slot_count, TV, TC, rank_span),
        val_sum.reshape(2, slot_count, TV, TV, rank_span),
        cond_sum.reshape(2, slot_count, TC, TC, rank_span),
        screen_part,
        coulomb_part,
    )
    kernel = jnp.where(live_tile, kernel, jnp.zeros_like(kernel))
    return lax.psum_scatter(
        kernel.astype(jnp.bfloat16), "ga", scatter_dimension=2, tiled=True
    ).astype(jnp.float32)


def solution(mesh):
    in_specs = (
        P(("vp", "cp"), "ga"),
        P(("vp", "cp"), "ga"),
        P("ga", None),
        P(),
        P(),
        P(),
        P(("vp", "cp")),
    )
    out_specs = P(None, ("vp", "cp"), "ga")
    return jax.shard_map(shards, mesh=mesh, in_specs=in_specs, out_specs=out_specs, check_vma=False)
```

profile of v0, /device:TPU:0, one launch (start us, length us, event | category | flops | bytes accessed | tf_op | source)
XLA Modules:
  0.0 302.0 jit_solution(14764287237343330676)
XLA Ops:
  6.5 0.0 all-gather.3.cloned.1.call-start
  6.5 0.7 all-gather.3.cloned.1.call-update
  7.3 0.0 all-gather.5.cloned.1.call-start
  7.3 0.7 all-gather.5.cloned.1.call-update
  8.0 0.0 reduce-scatter.10.cloned.1.call-start
  8.1 0.8 fusion.10
  8.8 0.1 iota_add_fusion
  8.9 0.1 add.77
  9.0 0.1 iota_add_fusion.1
  9.0 0.1 add.72
  9.1 48.2 %all-gather.3.cloned.1.call-done = bf16[512,6144]{1,0:T(8,128)(2,1)} async-done(((bf16[64,6144]{1,0:T(8,128)(2,1)}), bf16[512,6144]{1,0:T(8,128)(2,1)}) %all-gather.3.cloned.1.call-update) | async-done | bytes 6291472 | tf_op jit(solution)/shard_map/all_gather | solution.py:48
  57.4 4.0 %convolution_convert_fusion.1 = bf16[64,6144]{1,0:T(8,128)(2,1)S(1)} fusion(bf16[512,6144]{1,0:T(8,128)(2,1)} %all-gather.3.cloned.1.call-done, s32[64]{0:T(128)S(1)} %add.72), kind=kOutput, calls=%fused_computation.4 | convolution fusion | flops 403079168 | bytes 7078144 | tf_op jit(solution)/shard_map/dot_general | solution.py:15
  61.4 0.1 fusion.3
  61.5 43.1 %all-gather.5.cloned.1.call-done = bf16[512,6144]{1,0:T(8,128)(2,1)} async-done(((bf16[64,6144]{1,0:T(8,128)(2,1)}), bf16[512,6144]{1,0:T(8,128)(2,1)}) %all-gather.5.cloned.1.call-update) | async-done | bytes 6291472 | tf_op jit(solution)/shard_map/all_gather | solution.py:51
  104.7 4.0 %convolution_convert_fusion = bf16[64,6144]{1,0:T(8,128)(2,1)S(1)} fusion(bf16[512,6144]{1,0:T(8,128)(2,1)} %all-gather.5.cloned.1.call-done, s32[64]{0:T(128)S(1)} %add.77), kind=kOutput, calls=%fused_computation.3 | convolution fusion | flops 403079168 | bytes 7078144 | tf_op jit(solution)/shard_map/dot_general | solution.py:15
  108.7 0.1 fusion.2
  108.8 0.2 multiply_convert_fusion.3
  109.1 7.1 %convolution_convert_fusion.5 = bf16[128,1024]{1,0:T(8,128)(2,1)} fusion(bf16[128,6144]{1,0:T(8,128)(2,1)S(1)} %bitcast.71, bf16[6144,1024]{1,0:T(8,128)(2,1)} %param.9), kind=kOutput, calls=%fused_computation.10 | convolution fusion | flops 1610743808 | bytes 14417920 | tf_op jit(solution)/shard_map/dot_general | solution.py:67
  116.2 0.0 reduce-scatter.10.cloned.1.call-update
  116.2 0.0 reduce-scatter.14.cloned.1.call-start
  116.2 5.7 %multiply_convert_fusion = bf16[2,6,8,8,6144]{4,3,2,1,0:T(8,128)(2,1)} fusion(f32[6,8,6144]{2,1,0:T(8,128)S(1)} %fusion.3, f32[2,8,6144]{2,1,0:T(8,128)S(1)} %fusion.6), kind=kLoop, calls=%fused_computation | loop fusion | flops 9437184 | bytes 11010048 | tf_op jit(solution)/shard_map/convert_element_type | solution.py:23
  121.9 15.7 %convolution_convert_fusion.2 = bf16[768,1024]{1,0:T(8,128)(2,1)} fusion(bf16[768,6144]{1,0:T(8,128)(2,1)} %bitcast.73, bf16[6144,1024]{1,0:T(8,128)(2,1)} %param.9), kind=kOutput, calls=%fused_computation.7 | convolution fusion | flops 9664462848 | bytes 23592960 | tf_op jit(solution)/shard_map/dot_general | solution.py:69
  137.6 5.7 %multiply_convert_fusion.1 = bf16[2,6,8,8,6144]{4,3,2,1,0:T(8,128)(2,1)} fusion(f32[6,8,6144]{2,1,0:T(8,128)S(1)} %fusion.2, f32[2,8,6144]{2,1,0:T(8,128)S(1)} %fusion.5), kind=kLoop, calls=%fused_computation.1 | loop fusion | flops 9437184 | bytes 11010048 | tf_op jit(solution)/shard_map/convert_element_type | solution.py:23
  143.3 0.0 reduce-scatter.14.cloned.1.call-update
  143.3 0.2 reduce-scatter.12.cloned.1.call-start
  143.5 15.7 %convolution_convert_fusion.3 = bf16[768,1024]{1,0:T(8,128)(2,1)} fusion(bf16[768,6144]{1,0:T(8,128)(2,1)} %bitcast.72, bf16[6144,1024]{1,0:T(8,128)(2,1)} %param.9), kind=kOutput, calls=%fused_computation.8 | convolution fusion | flops 9664462848 | bytes 23592960 | tf_op jit(solution)/shard_map/dot_general | solution.py:70
  159.2 0.0 reduce-scatter.12.cloned.1.call-update
  159.2 0.0 reduce-scatter.8.cloned.1.call-start
  159.3 0.8 multiply_convert_fusion.2
  160.1 0.0 copy-start
  160.2 0.0 copy-start.1
  160.2 9.1 %convolution_convert_fusion.4 = bf16[384,1024]{1,0:T(8,128)(2,1)} fusion(bf16[384,6144]{1,0:T(8,128)(2,1)S(1)} %bitcast.75, bf16[6144,1024]{1,0:T(8,128)(2,1)} %param.9), kind=kOutput, calls=%fused_computation.9 | convolution fusion | flops 4832231424 | bytes 18087936 | tf_op jit(solution)/shard_map/dot_general | solution.py:68
  169.3 0.0 reduce-scatter.8.cloned.1.call-update
  169.3 0.3 reduce-scatter.16.cloned.1.call-start
  169.6 0.8 dynamic_slice.7
  170.3 0.8 dynamic_slice.6
  171.1 0.0 copy-done
  171.1 0.0 copy-done.1
  171.1 0.1 broadcast_compare_fusion
  171.2 0.0 reduce-scatter.10.cloned.1.call-done
  171.2 0.9 convert_multiply_fusion.2
  172.0 6.9 %reduce-scatter.14.cloned.1.call-done = bf16[768,256]{1,0:T(8,128)(2,1)} async-done(((bf16[768,1024]{1,0:T(8,128)(2,1)}), bf16[768,256]{1,0:T(8,128)(2,1)}) %reduce-scatter.14.cloned.1.call-update) | async-done | bytes 393232 | tf_op jit(solution)/shard_map/reduce_scatter | solution.py:82
  178.9 36.5 %reduce-scatter.12.cloned.1.call-done = bf16[768,256]{1,0:T(8,128)(2,1)} async-done(((bf16[768,1024]{1,0:T(8,128)(2,1)}), bf16[768,256]{1,0:T(8,128)(2,1)}) %reduce-scatter.12.cloned.1.call-update) | async-done | bytes 393232 | tf_op jit(solution)/shard_map/reduce_scatter | solution.py:85
  215.4 6.3 %fusion = f32[2,6,8,8,8,8]{5,3,4,2,1,0:T(8,128)} fusion(bf16[2,6,8,8,256,1]{4,3,5,2,1,0:T(8,128)(2,1)} %bitcast.78, bf16[2,6,8,8,256]{4,3,2,1,0:T(8,128)(2,1)} %bitcast.77, f32[256]{0:T(256)S(1)} %dynamic_slice.7), kind=kOutput, calls=%fused_computation.11 | convolution fusion | flops 151388160 | bytes 984064 | tf_op jit(solution)/shard_map/qsavr,qscdr->qsacvd/dot_general | solution.py:30
  221.6 4.3 %copy.11 = f32[2,6,8,8,8,8]{2,3,4,0,5,1:T(8,128)S(1)} copy(f32[2,6,8,8,8,8]{5,3,4,2,1,0:T(8,128)} %fusion) | data formatting | bytes 393216 | tf_op jit(solution)/shard_map/qsavr,qscdr->qsacvd/dot_general | solution.py:30
  226.0 13.6 %reduce-scatter.8.cloned.1.call-done = bf16[384,256]{1,0:T(8,128)(2,1)} async-done(((bf16[384,1024]{1,0:T(8,128)(2,1)}), bf16[384,256]{1,0:T(8,128)(2,1)}) %reduce-scatter.8.cloned.1.call-update) | async-done | bytes 196624 | tf_op jit(solution)/shard_map/reduce_scatter | solution.py:79
  239.6 3.5 %bitcast_subtract_fusion = bf16[2,6,8,8,8,8]{3,5,2,0,4,1:T(8,128)(2,1)} fusion(f32[2,6,8,8,8,8]{2,3,4,0,5,1:T(8,128)S(1)} %copy.11, bf16[6,8,8,256,1,1]{3,2,5,4,1,0:T(8,128)(2,1)} %bitcast.79, f32[2,8,8,256,1,1]{3,2,1,0,5,4:T(8,128)S(1)} %bitcast.76), kind=kOutput, calls=%fused_computation.5 | convolution fusion | flops 151142400 | bytes 622592 | tf_op jit(solution)/shard_map/qacr,svdr->qsacvd/dot_general | solution.py:27
  243.0 2.1 copy.12
  245.2 1.7 reshape.286
  246.8 0.1 select_convert_fusion
  247.0 7.4 %copy.17 = bf16[2,6,4096]{0,1,2:T(8,128)(2,1)} copy(bf16[2,6,4096]{2,0,1:T(2,128)(2,1)S(1)} %select_convert_fusion) | data formatting | bytes 196608
  254.4 9.5 %reshape.297 = bf16[4096,12]{1,0:T(8,128)(2,1)} reshape(bf16[4096,6,2]{2,1,0:T(8,128)(2,1)} %bitcast.70) | data formatting | bytes 196608
  263.9 0.0 reduce-scatter.16.cloned.1.call-update
  263.9 27.0 %reduce-scatter.16.cloned.1.call-done = bf16[1024,12]{1,0:T(8,128)(2,1)} async-done(((bf16[4096,12]{1,0:T(8,128)(2,1)}), bf16[1024,12]{1,0:T(8,128)(2,1)}) %reduce-scatter.16.cloned.1.call-update) | async-done | bytes 24592
  290.9 2.4 reshape.298
  293.3 1.2 copy.18
  294.5 0.6 convert_element_type.152
  (3 shorter events, 0.1 us)
Async XLA Ops:
  6.5 50.8 %all-gather.3.cloned.1.call-start = ((), (), s32[]{:S(2)}) async-start(), calls=%async_computation.5 | async-start | bytes 7077888 | tf_op jit(solution)/shard_map/all_gather | solution.py:48
  7.3 97.4 %all-gather.5.cloned.1.call-start = ((), (), s32[]{:S(2)}) async-start(), calls=%async_computation.6 | async-start | bytes 7077888 | tf_op jit(solution)/shard_map/all_gather | solution.py:51
  8.0 163.2 %reduce-scatter.10.cloned.1.call-start = ((), (), s32[]{:S(2)}) async-start(), calls=%async_computation.8 | async-start | bytes 327680 | tf_op jit(solution)/shard_map/reduce_scatter | solution.py:76
  116.2 62.7 %reduce-scatter.14.cloned.1.call-start = ((), (), s32[]{:S(2)}) async-start(), calls=%async_computation.10 | async-start | bytes 1966080 | tf_op jit(solution)/shard_map/reduce_scatter | solution.py:82
  143.3 72.1 %reduce-scatter.12.cloned.1.call-start = ((), (), s32[]{:S(2)}) async-start(), calls=%async_computation.9 | async-start | bytes 1966080 | tf_op jit(solution)/shard_map/reduce_scatter | solution.py:85
  159.2 80.3 %reduce-scatter.8.cloned.1.call-start = ((), (), s32[]{:S(2)}) async-start(), calls=%async_computation.7 | async-start | bytes 983040 | tf_op jit(solution)/shard_map/reduce_scatter | solution.py:79
  160.1 10.9 %copy-start = (s32[6]{0:T(128)S(1)}, s32[6]{0:T(128)}, u32[]{:S(2)}) copy-start(s32[6]{0:T(128)} %param.13) | copy-start | bytes 76
  160.2 10.9 %copy-start.1 = (s32[2]{0:T(128)S(1)}, s32[2]{0:T(128)}, u32[]{:S(2)}) copy-start(s32[2]{0:T(128)} %param.12) | copy-start | bytes 28
  169.3 121.6 %reduce-scatter.16.cloned.1.call-start = ((), (), s32[]{:S(2)}) async-start(), calls=%async_computation.11 | async-start | bytes 1310720
Sparse Core Ops, SparseCore 0:
  9.2 48.1 all-gather.2
  59.2 45.3 all-gather.4
  116.3 19.9 reduce-scatter.9
  143.4 35.4 reduce-scatter.13
  181.0 34.2 reduce-scatter.11
  217.5 21.9 reduce-scatter.7
  264.0 26.8 reduce-scatter.15
where the time goes:
time: 303 us; the launch traced here: 302 us
  waiting for transfers between devices  177 us (58%)
  matrix products  65.4 us (22%)
  local copies, waits for them, and re-layouts  30.3 us (10%)
  other arithmetic  15.2 us (5%)
  between operations  13.6 us (4%)
    all_gather x1, waiting for transfers between devices, shards(): lax.all_gather(valence_wavefunction, ('vp', 'cp'), axis=0, tiled=True)  48.2 us
    all_gather x1, waiting for transfers between devices, shards(): lax.all_gather(cond_wave, ('vp', 'cp'), axis=0, tiled=True)  43.1 us
    reduce_scatter x1, waiting for transfers between devices, shards(): lax.psum_scatter(cond_part.astype(jnp.bfloat16), 'ga', scatter_dimension=...  36.5 us
    unnamed x8, waiting for transfers between devices  28.5 us
    unnamed x8, local copies, waits for them, and re-layouts  20.5 us
    dot_general x1, matrix products, shards(): jnp.dot(cond_rho, screen_basis, preferred_element_type=jnp.float32)  15.7 us
    dot_general x1, matrix products, shards(): jnp.dot(val_rho, screen_basis, preferred_element_type=jnp.float32)  15.7 us
    reduce_scatter x1, waiting for transfers between devices, shards(): lax.psum_scatter(col_part.astype(jnp.bfloat16), 'ga', scatter_dimension=1...  13.6 us
  transfers between devices with their start and end apart: 7, of which 6 were waited for; matrix products, arithmetic and copies ran while one was open for 23% of the time, Pallas kernels for 0%

commit v1 on v0

--- a/solution.py
+++ b/solution.py
@@ -7,6 +7,11 @@
 TV = 8
 TC = 8
 NCT = 64
+
+
+def gather_over(x, axis, dim):
+    stack = jnp.stack([x] * lax.axis_size(axis))
+    return jnp.concatenate(lax.all_to_all(stack, axis, 0, 0), axis=dim)
 
 
 def select_bands(wanted, shard_part):
@@ -44,9 +49,7 @@
     conduction_wanted = (
         (pair_tiles % NCT)[:, None] * TC + jnp.arange(TC, dtype=jnp.int32)[None, :]
     ).reshape(-1)
-    picked_val = select_bands(
-        val_wanted, lax.all_gather(valence_wavefunction, ("vp", "cp"), axis=0, tiled=True)
-    )
+    picked_val = select_bands(val_wanted, gather_over(valence_wavefunction, ("vp", "cp"), 0))
     picked_cond = select_bands(
         conduction_wanted, lax.all_gather(cond_wave, ("vp", "cp"), axis=0, tiled=True)
     )

time: 303 us -> 316 us (1.043)
  starting transfers between devices: 0.65 us -> 5.94 us
  local copies, waits for them, and re-layouts: 30.3 us -> 34.9 us
    all_to_all x0 -> x1, waiting for transfers between devices: none -> 96.7 us  [gather_over(): return jnp.concatenate(lax.all_to_all(stack, axis, 0, 0), axis=dim)]
    all_gather x1 -> x0, waiting for transfers between devices: 48.2 us -> none  [shards(): lax.all_gather(valence_wavefunction, ('vp', 'cp'), axis=0, tiled=True)]
    all_gather x1, waiting for transfers between devices: 43.1 us -> 0.01 us  [shards(): lax.all_gather(cond_wave, ('vp', 'cp'), axis=0, tiled=True)]
    all_to_all x0 -> x1, starting transfers between devices: none -> 5.33 us  [gather_over(): return jnp.concatenate(lax.all_to_all(stack, axis, 0, 0), axis=dim)]
    another operation x0 -> x1, local copies, waits for them, and re-layouts: none -> 4.55 us  [gather_over(): stack = jnp.stack([x] * lax.axis_size(axis))]
    unnamed x8 -> x7, waiting for transfers between devices: 28.5 us -> 27.7 us
  transfers between devices with their start and end apart: 7 -> 7, of which waited for: 6 -> 5; matrix products, arithmetic and copies ran while one was open for 23% -> 24% of each run, Pallas kernels for 0% -> 0%
where the time goes in v1:
time: 316 us; the launch traced here: 315 us
  waiting for transfers between devices  180 us (57%)
  matrix products  65.6 us (21%)
  local copies, waits for them, and re-layouts  34.9 us (11%)
  other arithmetic  14.5 us (5%)
  between operations  13.6 us (4%)
  starting transfers between devices  5.94 us (2%)
    all_to_all x1, waiting for transfers between devices, gather_over(): return jnp.concatenate(lax.all_to_all(stack, axis, 0, 0), axis=dim)  96.7 us
    reduce_scatter x1, waiting for transfers between devices, shards(): lax.psum_scatter(cond_part.astype(jnp.bfloat16), 'ga', scatter_dimension=...  36.5 us
    unnamed x7, waiting for transfers between devices  27.7 us
    unnamed x8, local copies, waits for them, and re-layouts  20.5 us
    dot_general x1, matrix products, shards(): jnp.dot(val_rho, screen_basis, preferred_element_type=jnp.float32)  15.7 us
    dot_general x1, matrix products, shards(): jnp.dot(cond_rho, screen_basis, preferred_element_type=jnp.float32)  15.7 us
    reduce_scatter x1, waiting for transfers between devices, shards(): lax.psum_scatter(col_part.astype(jnp.bfloat16), 'ga', scatter_dimension=1...  13.5 us
    convert_element_type x4, other arithmetic, outer_rows(): return product.astype(jnp.bfloat16)  12.4 us
  transfers between devices with their start and end apart: 7, of which 5 were waited for; matrix products, arithmetic and copies ran while one was open for 24% of the time, Pallas kernels for 0%

profile of v1, /device:TPU:0, one launch (start us, length us, event | category | flops | bytes accessed | tf_op | source)
XLA Modules:
  0.0 315.0 jit_solution(9522621604737508078)
XLA Ops:
  6.5 0.0 all-gather.2.cloned.1.call-start
  6.5 0.7 all-gather.2.cloned.1.call-update
  7.3 4.5 %stack.2 = bf16[8,64,6144]{2,1,0:T(8,128)(2,1)} broadcast(bf16[64,6144]{1,0:T(8,128)(2,1)} %param.7), dimensions={1,2} | broadcast | bytes 7077888 | tf_op jit(solution)/shard_map/stack | solution.py:13
  11.8 0.0 copy-start
  11.8 0.0 copy-start.1
  11.8 5.3 %all-to-all-start = ((bf16[8,64,6144]{2,1,0:T(8,128)(2,1)}), bf16[8,64,6144]{2,1,0:T(8,128)(2,1)}, u32[]{:S(2)}, u32[]{:S(2)}) async-start(bf16[8,64,6144]{2,1,0:T(8,128)(2,1)} %stack.2), calls=%async_computation | async-start | bytes 12582912 | tf_op jit(solution)/shard_map/all_to_all | solution.py:14
  17.1 0.0 reduce-scatter.10.cloned.1.call-start
  17.2 0.0 copy-done
  17.2 0.0 copy-done.1
  17.2 0.1 fusion.10
  17.3 0.1 iota_add_fusion
  17.4 0.1 add.77
  17.4 0.1 iota_add_fusion.1
  17.5 0.1 add.72
  17.6 96.7 %all-to-all-done = bf16[8,64,6144]{2,1,0:T(8,128)(2,1)} async-done(((bf16[8,64,6144]{2,1,0:T(8,128)(2,1)}), bf16[8,64,6144]{2,1,0:T(8,128)(2,1)}, u32[]{:S(2)}, u32[]{:S(2)}) %all-to-all-start) | async-done | bytes 6291488 | tf_op jit(solution)/shard_map/all_to_all | solution.py:14
  114.3 4.0 %convolution_convert_fusion.1 = bf16[64,6144]{1,0:T(8,128)(2,1)S(1)} fusion(bf16[512,6144]{1,0:T(8,128)(2,1)} %bitcast, s32[64]{0:T(128)S(1)} %add.72), kind=kOutput, calls=%fused_computation.4 | convolution fusion | flops 403079168 | bytes 7078144 | tf_op jit(solution)/shard_map/dot_general | solution.py:20
  118.3 0.1 fusion.3
  118.4 5.7 %multiply_convert_fusion = bf16[2,6,8,8,6144]{4,3,2,1,0:T(8,128)(2,1)} fusion(f32[6,8,6144]{2,1,0:T(8,128)S(1)} %fusion.3, f32[2,8,6144]{2,1,0:T(8,128)S(1)} %fusion.6), kind=kLoop, calls=%fused_computation | loop fusion | flops 9437184 | bytes 11010048 | tf_op jit(solution)/shard_map/convert_element_type | solution.py:28
  124.1 0.0 all-gather.2.cloned.1.call-done
  124.1 4.0 %convolution_convert_fusion = bf16[64,6144]{1,0:T(8,128)(2,1)S(1)} fusion(bf16[512,6144]{1,0:T(8,128)(2,1)} %all-gather.2.cloned.1.call-done, s32[64]{0:T(128)S(1)} %add.77), kind=kOutput, calls=%fused_computation.3 | convolution fusion | flops 403079168 | bytes 7078144 | tf_op jit(solution)/shard_map/dot_general | solution.py:20
  128.2 0.2 multiply_convert_fusion.3
  128.4 7.1 %convolution_convert_fusion.5 = bf16[128,1024]{1,0:T(8,128)(2,1)} fusion(bf16[128,6144]{1,0:T(8,128)(2,1)S(1)} %bitcast.72, bf16[6144,1024]{1,0:T(8,128)(2,1)} %param.9), kind=kOutput, calls=%fused_computation.10 | convolution fusion | flops 1610743808 | bytes 14417920 | tf_op jit(solution)/shard_map/dot_general | solution.py:70
  135.5 0.0 reduce-scatter.10.cloned.1.call-update
  135.5 0.0 reduce-scatter.14.cloned.1.call-start
  135.6 15.7 %convolution_convert_fusion.2 = bf16[768,1024]{1,0:T(8,128)(2,1)} fusion(bf16[768,6144]{1,0:T(8,128)(2,1)} %bitcast.73, bf16[6144,1024]{1,0:T(8,128)(2,1)} %param.9), kind=kOutput, calls=%fused_computation.7 | convolution fusion | flops 9664462848 | bytes 23592960 | tf_op jit(solution)/shard_map/dot_general | solution.py:72
  151.3 0.0 reduce-scatter.14.cloned.1.call-update
  151.3 0.2 reduce-scatter.12.cloned.1.call-start
  151.6 0.1 fusion.2
  151.7 5.7 %multiply_convert_fusion.1 = bf16[2,6,8,8,6144]{4,3,2,1,0:T(8,128)(2,1)} fusion(f32[6,8,6144]{2,1,0:T(8,128)S(1)} %fusion.2, f32[2,8,6144]{2,1,0:T(8,128)S(1)} %fusion.5), kind=kLoop, calls=%fused_computation.1 | loop fusion | flops 9437184 | bytes 11010048 | tf_op jit(solution)/shard_map/convert_element_type | solution.py:28
  157.3 15.7 %convolution_convert_fusion.3 = bf16[768,1024]{1,0:T(8,128)(2,1)} fusion(bf16[768,6144]{1,0:T(8,128)(2,1)} %bitcast.74, bf16[6144,1024]{1,0:T(8,128)(2,1)} %param.9), kind=kOutput, calls=%fused_computation.8 | convolution fusion | flops 9664462848 | bytes 23592960 | tf_op jit(solution)/shard_map/dot_general | solution.py:73
  173.0 0.0 reduce-scatter.12.cloned.1.call-update
  173.0 0.0 reduce-scatter.8.cloned.1.call-start
  173.0 0.8 multiply_convert_fusion.2
  173.9 9.1 %convolution_convert_fusion.4 = bf16[384,1024]{1,0:T(8,128)(2,1)} fusion(bf16[384,6144]{1,0:T(8,128)(2,1)S(1)} %bitcast.76, bf16[6144,1024]{1,0:T(8,128)(2,1)} %param.9), kind=kOutput, calls=%fused_computation.9 | convolution fusion | flops 4832231424 | bytes 18087936 | tf_op jit(solution)/shard_map/dot_general | solution.py:71
  183.0 0.0 reduce-scatter.8.cloned.1.call-update
  183.0 0.3 reduce-scatter.16.cloned.1.call-start
  183.3 0.8 dynamic_slice.7
  184.1 0.8 dynamic_slice.6
  184.8 0.1 broadcast_compare_fusion
  184.9 0.0 reduce-scatter.10.cloned.1.call-done
  184.9 0.9 convert_multiply_fusion.2
  185.8 6.1 %reduce-scatter.14.cloned.1.call-done = bf16[768,256]{1,0:T(8,128)(2,1)} async-done(((bf16[768,1024]{1,0:T(8,128)(2,1)}), bf16[768,256]{1,0:T(8,128)(2,1)}) %reduce-scatter.14.cloned.1.call-update) | async-done | bytes 393232 | tf_op jit(solution)/shard_map/reduce_scatter | solution.py:85
  191.9 36.5 %reduce-scatter.12.cloned.1.call-done = bf16[768,256]{1,0:T(8,128)(2,1)} async-done(((bf16[768,1024]{1,0:T(8,128)(2,1)}), bf16[768,256]{1,0:T(8,128)(2,1)}) %reduce-scatter.12.cloned.1.call-update) | async-done | bytes 393232 | tf_op jit(solution)/shard_map/reduce_scatter | solution.py:88
  228.3 6.3 %fusion = f32[2,6,8,8,8,8]{5,3,4,2,1,0:T(8,128)} fusion(bf16[2,6,8,8,256,1]{4,3,5,2,1,0:T(8,128)(2,1)} %bitcast.79, bf16[2,6,8,8,256]{4,3,2,1,0:T(8,128)(2,1)} %bitcast.78, f32[256]{0:T(256)S(1)} %dynamic_slice.7), kind=kOutput, calls=%fused_computation.11 | convolution fusion | flops 151388160 | bytes 984064 | tf_op jit(solution)/shard_map/qsavr,qscdr->qsacvd/dot_general | solution.py:35
  234.7 4.3 %copy.11 = f32[2,6,8,8,8,8]{2,3,4,0,5,1:T(8,128)S(1)} copy(f32[2,6,8,8,8,8]{5,3,4,2,1,0:T(8,128)} %fusion) | data formatting | bytes 393216 | tf_op jit(solution)/shard_map/qsavr,qscdr->qsacvd/dot_general | solution.py:35
  239.0 13.5 %reduce-scatter.8.cloned.1.call-done = bf16[384,256]{1,0:T(8,128)(2,1)} async-done(((bf16[384,1024]{1,0:T(8,128)(2,1)}), bf16[384,256]{1,0:T(8,128)(2,1)}) %reduce-scatter.8.cloned.1.call-update) | async-done | bytes 196624 | tf_op jit(solution)/shard_map/reduce_scatter | solution.py:82
  252.5 3.6 %bitcast_subtract_fusion = bf16[2,6,8,8,8,8]{3,5,2,0,4,1:T(8,128)(2,1)} fusion(f32[2,6,8,8,8,8]{2,3,4,0,5,1:T(8,128)S(1)} %copy.11, bf16[6,8,8,256,1,1]{3,2,5,4,1,0:T(8,128)(2,1)} %bitcast.80, f32[2,8,8,256,1,1]{3,2,1,0,5,4:T(8,128)S(1)} %bitcast.77), kind=kOutput, calls=%fused_computation.5 | convolution fusion | flops 151142400 | bytes 622592 | tf_op jit(solution)/shard_map/qacr,svdr->qsacvd/dot_general | solution.py:32
  256.1 2.1 copy.12
  258.2 1.7 reshape.292
  259.9 0.1 select_convert_fusion
  260.0 7.4 %copy.17 = bf16[2,6,4096]{0,1,2:T(8,128)(2,1)} copy(bf16[2,6,4096]{2,0,1:T(2,128)(2,1)S(1)} %select_convert_fusion) | data formatting | bytes 196608
  267.4 9.5 %reshape.303 = bf16[4096,12]{1,0:T(8,128)(2,1)} reshape(bf16[4096,6,2]{2,1,0:T(8,128)(2,1)} %bitcast.71) | data formatting | bytes 196608
  276.9 0.0 reduce-scatter.16.cloned.1.call-update
  277.0 26.9 %reduce-scatter.16.cloned.1.call-done = bf16[1024,12]{1,0:T(8,128)(2,1)} async-done(((bf16[4096,12]{1,0:T(8,128)(2,1)}), bf16[1024,12]{1,0:T(8,128)(2,1)}) %reduce-scatter.16.cloned.1.call-update) | async-done | bytes 24592
  303.9 2.4 reshape.304
  306.3 1.2 copy.18
  307.5 0.6 convert_element_type.152
  (3 shorter events, 0.1 us)
Async XLA Ops:
  6.5 117.5 %all-gather.2.cloned.1.call-start = ((), (), s32[]{:S(2)}) async-start(), calls=%async_computation.6 | async-start | bytes 7077888 | tf_op jit(solution)/shard_map/all_gather | solution.py:54
  11.8 5.4 %copy-start = (s32[6]{0:T(128)S(1)}, s32[6]{0:T(128)}, u32[]{:S(2)}) copy-start(s32[6]{0:T(128)} %param.13) | copy-start | bytes 76
  11.8 5.4 %copy-start.1 = (s32[2]{0:T(128)S(1)}, s32[2]{0:T(128)}, u32[]{:S(2)}) copy-start(s32[2]{0:T(128)} %param.12) | copy-start | bytes 28
  11.8 102.5 %all-to-all-start = ((bf16[8,64,6144]{2,1,0:T(8,128)(2,1)}), bf16[8,64,6144]{2,1,0:T(8,128)(2,1)}, u32[]{:S(2)}, u32[]{:S(2)}) async-start(bf16[8,64,6144]{2,1,0:T(8,128)(2,1)} %stack.2), calls=%async_computation | async-start | bytes 12582912 | tf_op jit(solution)/shard_map/all_to_all | solution.py:14
  17.1 167.8 %reduce-scatter.10.cloned.1.call-start = ((), (), s32[]{:S(2)}) async-start(), calls=%async_computation.8 | async-start | bytes 327680 | tf_op jit(solution)/shard_map/reduce_scatter | solution.py:79
  135.5 56.3 %reduce-scatter.14.cloned.1.call-start = ((), (), s32[]{:S(2)}) async-start(), calls=%async_computation.10 | async-start | bytes 1966080 | tf_op jit(solution)/shard_map/reduce_scatter | solution.py:85
  151.3 77.0 %reduce-scatter.12.cloned.1.call-start = ((), (), s32[]{:S(2)}) async-start(), calls=%async_computation.9 | async-start | bytes 1966080 | tf_op jit(solution)/shard_map/reduce_scatter | solution.py:88
  173.0 79.5 %reduce-scatter.8.cloned.1.call-start = ((), (), s32[]{:S(2)}) async-start(), calls=%async_computation.7 | async-start | bytes 983040 | tf_op jit(solution)/shard_map/reduce_scatter | solution.py:82
  183.0 120.8 %reduce-scatter.16.cloned.1.call-start = ((), (), s32[]{:S(2)}) async-start(), calls=%async_computation.11 | async-start | bytes 1310720
Sparse Core Ops, SparseCore 0:
  9.2 89.2 all-gather.1
  135.7 20.1 reduce-scatter.9
  158.2 33.6 reduce-scatter.13
  194.0 34.2 reduce-scatter.11
  230.5 21.9 reduce-scatter.7
  277.1 26.7 reduce-scatter.15
